TPU v7x, 128 devices: a whole 4x4x4 slice. The times are simulated.
128 devices in a mesh: row: 8 (over y, core), col: 16 (over z, x).
Axes of the slice: x: 4, y: 4, z: 4, core: 2. Of those that a mesh axis runs over, the one named last changes fastest.
Arguments:
- ancestor_inverse: float32 [12288, 12288], P('row', 'col')
- factor: bfloat16 [3, 12288, 512], P(None, ('row', 'col')), may hold values from -0.5 to 0.5
- coupling: float32 [3, 512, 512], replicated, may hold values from -0.25 to 0.25
- diagonal_inverse: float32 [3, 512, 512], replicated, may hold values from -6 to 6
- ancestors: int32 [3, 24], replicated, may hold values from -1 to 23, as said below
Outputs:
- block_columns: float32 [3, 12288, 512], P(None, ('row', 'col'))
- block_rows: float32 [3, 12288, 512], P(None, ('col', 'row'))
- node_blocks: float32 [3, 3, 512, 512], replicated
Inputs may be any that keep to these rules, and one draw needn't show every extreme that they name: `ancestors`: row k lists the ancestor block rows of supernode k, blocks of 512 rows: distinct indices in increasing order, then -1 in the slots left. Every block is listed by some supernode.
All inputs are finite; a program needn't handle non-finite values.
Results may differ from a plain program's by a relative error of at most 0.0003.
Values may be sent and summed in bfloat16 or wider, within the bound.
A program may use at most 128 MiB of HBM per device.

v0:
```python
import jax
import jax.numpy as jnp
from jax import lax
from jax.sharding import PartitionSpec as P

highest = lax.Precision.HIGHEST


def broadcast(value, axis, source):
    kept = jnp.where(lax.axis_index(axis) == source, value, 0).astype(value.dtype)
    return lax.psum(kept, axis)


def matmul(left, right):
    return jnp.dot(left, right, precision=highest)


def left_dot(left, right):
    return lax.dot_general(left, right, (((0,), (0,)), ((), ())), precision=highest)


def pair_index(later, earlier):
    return later * (later - 1) // 2 + earlier


def local(ancestor_inverse, factor, coupling, diagonal_inverse, ancestors):
    col_count = lax.axis_size("col")
    row_count = lax.axis_size("row")
    row_index = lax.axis_index("row")
    col_index = lax.axis_index("col")
    nodes_total, piece_rows, sn_width = factor.shape
    rows_here, cols_here = ancestor_inverse.shape
    group_ratio = rows_here // cols_here
    first_row = (row_index * col_count + col_index) * piece_rows
    block_of_row = (first_row + jnp.arange(piece_rows, dtype=jnp.int32)) // sn_width
    source_row = col_index // group_ratio
    block_start = col_index % group_ratio * cols_here
    row_layout = []
    solved = {}
    for current in range(nodes_total):
        listed = jnp.any(ancestors[current][:, None] == block_of_row[None, :], axis=0)
        lower_part = jnp.where(listed[:, None], factor[current], jnp.zeros_like(factor[current]))
        lower_rows = lax.all_gather(lower_part, "col", axis=0, tiled=True)
        own_block = lax.dynamic_slice_in_dim(lower_rows, block_start, cols_here, 0)
        lower_cols = broadcast(own_block, "row", source_row).astype(jnp.float32)
        lower_here = lower_part.astype(jnp.float32)
        product_sum = lax.psum_scatter(
            matmul(ancestor_inverse, lower_cols), "col", scatter_dimension=0, tiled=True
        )
        for earlier in range(current):
            product_sum = product_sum + matmul(
                row_layout[earlier], coupling[pair_index(current, earlier)]
            )
        column = -product_sum
        stacked = jnp.concatenate(row_layout + [column], axis=1)
        summed = lax.psum(left_dot(lower_here, stacked), ("row", "col"))
        crosses = [
            summed[:, earlier * sn_width : (earlier + 1) * sn_width] for earlier in range(current)
        ]
        self_term = summed[:, current * sn_width : (current + 1) * sn_width]
        for earlier in range(current):
            block_value = -crosses[earlier].T
            for inner in range(current):
                block_value = block_value - matmul(
                    solved[earlier, inner], coupling[pair_index(current, inner)]
                )
            solved[earlier, current] = block_value
            solved[current, earlier] = block_value.T
        diag_value = diagonal_inverse[current] - self_term
        for earlier in range(current):
            diag_value = diag_value - left_dot(
                coupling[pair_index(current, earlier)], solved[earlier, current]
            )
        solved[current, current] = diag_value
        row_layout.append(column)
    finished = jnp.stack(row_layout)
    part_rows = piece_rows // row_count
    ratio_cols = col_count // row_count
    split_parts = finished.reshape(nodes_total, row_count, part_rows, sn_width)
    held = lax.all_to_all(split_parts, "row", split_axis=1, concat_axis=1, tiled=True)
    targets = jnp.arange(row_count, dtype=jnp.int32) * ratio_cols + col_index // row_count
    onehot = (targets[:, None] == jnp.arange(col_count, dtype=jnp.int32)[None, :]).astype(
        jnp.float32
    )
    slotted = jnp.einsum("rc,nrqs->ncqs", onehot, held, precision=highest)
    arrived = lax.all_to_all(slotted, "col", split_axis=1, concat_axis=1, tiled=True)
    picked = lax.dynamic_slice_in_dim(arrived, col_index % ratio_cols * row_count, row_count, 1)
    landed = lax.all_to_all(picked, "row", split_axis=1, concat_axis=1, tiled=True)
    mirrored_all = landed.reshape(nodes_total, piece_rows, sn_width)
    node_blocks = jnp.stack(
        [
            jnp.stack([solved[first_node, second_node] for second_node in range(nodes_total)])
            for first_node in range(nodes_total)
        ]
    )
    return (finished, mirrored_all, node_blocks)


def solution(mesh):
    placed = (P("row", "col"), P(None, ("row", "col"), None), P(), P(), P())
    return jax.shard_map(
        local,
        mesh=mesh,
        in_specs=placed,
        out_specs=(P(None, ("row", "col"), None), P(None, ("col", "row"), None), P()),
        check_vma=False,
    )
```

profile of v0, /device:TPU:1, one launch (start us, length us, event | category | flops | bytes accessed | tf_op | source)
XLA Modules:
  0.0 691.0 jit_solution(10552824575240240170)
XLA Ops:
  11.5 45.6 %all-gather.6.cloned.1.call-done = bf16[1536,512]{1,0:T(8,128)(2,1)} async-done(((bf16[96,512]{1,0:T(8,128)(2,1)}), bf16[1536,512]{1,0:T(8,128)(2,1)}) %all-gather.6.cloned.1.call-update) | async-done | bytes 1572880 | tf_op jit(solution)/shard_map/all_gather | solution.py:43
  59.2 43.3 %all-gather.4.cloned.1.call-done = bf16[1536,512]{1,0:T(8,128)(2,1)} async-done(((bf16[96,512]{1,0:T(8,128)(2,1)}), bf16[1536,512]{1,0:T(8,128)(2,1)}) %all-gather.4.cloned.1.call-update) | async-done | bytes 1572880 | tf_op jit(solution)/shard_map/all_gather | solution.py:43
  104.7 43.3 %all-gather.8.cloned.1.call-done = bf16[1536,512]{1,0:T(8,128)(2,1)} async-done(((bf16[96,512]{1,0:T(8,128)(2,1)}), bf16[1536,512]{1,0:T(8,128)(2,1)}) %all-gather.8.cloned.1.call-update) | async-done | bytes 1572880 | tf_op jit(solution)/shard_map/all_gather | solution.py:43
  150.3 66.0 %all-reduce.7.cloned.1.call-done = (bf16[768,512]{1,0:T(8,128)(2,1)}, bf16[768,512]{1,0:T(8,128)(2,1)}, bf16[768,512]{1,0:T(8,128)(2,1)}) async-done(((bf16[768,512]{1,0:T(8,128)(2,1)}, bf16[768,512]{1,0:T(8,128)(2,1)}, bf16[768,512]{1,0:T(8,128)(2,1)}), (bf16[768,512]{1,0:T(8,128)(2,1)}, bf16[768,512]{1,0:T(8,128)(2,1)}, bf16[768,512]{1,0:T(8,128)(2,1)})) %all-reduce.7.cloned.1.call-update) | async-done | bytes 2359312 | tf_op jit(solution)/shard_map/psum | solution.py:11
  216.2 6.7 convolution_bitcast_fusion.2
  225.3 6.7 convolution_bitcast_fusion.1
  234.5 6.7 convolution_bitcast_fusion
  244.1 57.1 %reduce-scatter.10.cloned.1.call-done = f32[96,512]{1,0:T(8,128)} async-done(((f32[1536,512]{1,0:T(8,128)}), f32[96,512]{1,0:T(8,128)}) %reduce-scatter.10.cloned.1.call-update) | async-done | bytes 196624 | tf_op jit(solution)/shard_map/reduce_scatter | solution.py:47
  301.2 78.3 %reduce-scatter.12.cloned.1.call-done = f32[96,512]{1,0:T(8,128)} async-done(((f32[1536,512]{1,0:T(8,128)}), f32[96,512]{1,0:T(8,128)}) %reduce-scatter.12.cloned.1.call-update) | async-done | bytes 196624 | tf_op jit(solution)/shard_map/reduce_scatter | solution.py:47
  381.3 77.3 %reduce-scatter.14.cloned.1.call-done = f32[96,512]{1,0:T(8,128)} async-done(((f32[1536,512]{1,0:T(8,128)}), f32[96,512]{1,0:T(8,128)}) %reduce-scatter.14.cloned.1.call-update) | async-done | bytes 196624 | tf_op jit(solution)/shard_map/reduce_scatter | solution.py:47
  464.2 3.1 fusion.38
  475.2 6.7 all-to-all-start
  481.9 15.6 %all-to-all-done = f32[3,8,12,512]{3,2,0,1:T(8,128)} async-done(((f32[3,8,12,512]{3,2,0,1:T(8,128)}), f32[3,8,12,512]{3,2,0,1:T(8,128)}, u32[]{:S(2)}, u32[]{:S(2)}) %all-to-all-start) | async-done | bytes 589856 | tf_op jit(solution)/shard_map/all_to_all | solution.py:80
  501.5 4.8 all-to-all-start.1
  506.3 21.0 %all-to-all-done.1 = f32[3,16,12,512]{3,2,0,1:T(8,128)} async-done(((f32[3,16,12,512]{3,2,0,1:T(8,128)}), f32[3,16,12,512]{3,2,0,1:T(8,128)}, u32[]{:S(2)}, u32[]{:S(2)}) %all-to-all-start.1) | async-done | bytes 1179680 | tf_op jit(solution)/shard_map/all_to_all | solution.py:86
  529.4 9.0 %all-to-all-start.2 = ((f32[3,8,12,512]{3,2,0,1:T(8,128)}), f32[3,8,12,512]{3,2,0,1:T(8,128)}, u32[]{:S(2)}, u32[]{:S(2)}) async-start(f32[3,8,12,512]{3,2,0,1:T(8,128)} %constant_dynamic-slice_fusion), calls=%async_computation.2 | async-start | bytes 1572864 | tf_op jit(solution)/shard_map/all_to_all | solution.py:88
  545.1 5.7 all-to-all-done.2
  555.1 83.9 %all-reduce.5.cloned.1.call-done = (f32[512,1536]{1,0:T(8,128)}, f32[512,512]{1,0:T(8,128)}, f32[512,1024]{0,1:T(8,128)}) async-done(((f32[512,1536]{1,0:T(8,128)}, f32[512,512]{1,0:T(8,128)}, f32[512,1024]{0,1:T(8,128)}), (f32[512,1536]{1,0:T(8,128)}, f32[512,512]{1,0:T(8,128)}, f32[512,1024]{0,1:T(8,128)})) %all-reduce.5.cloned.1.call-update) | async-done | bytes 6291472 | tf_op jit(solution)/shard_map/psum | solution.py:56
  638.9 3.8 bitcast_subtract_fusion.7
  653.7 3.1 fusion.2
  663.9 3.8 maximum_bitcast_fusion.1
  667.8 3.6 copy.95
  671.3 4.3 fusion.1
  679.1 4.9 pad_maximum_fusion
  (102 shorter events, 72.2 us)
Async XLA Ops:
  7.2 49.9 %all-gather.6.cloned.1.call-start = ((), (), s32[]{:S(2)}) async-start(), calls=%async_computation.7 | async-start | bytes 1671168 | tf_op jit(solution)/shard_map/all_gather | solution.py:43
  9.9 92.6 %all-gather.4.cloned.1.call-start = ((), (), s32[]{:S(2)}) async-start(), calls=%async_computation.6 | async-start | bytes 1671168 | tf_op jit(solution)/shard_map/all_gather | solution.py:43
  10.7 137.4 %all-gather.8.cloned.1.call-start = ((), (), s32[]{:S(2)}) async-start(), calls=%async_computation.8 | async-start | bytes 1671168 | tf_op jit(solution)/shard_map/all_gather | solution.py:43
  11.4 204.8 %all-reduce.7.cloned.1.call-start = ((), (), s32[]{:S(2)}) async-start(), calls=%async_computation.13 | async-start | bytes 4718592 | tf_op jit(solution)/shard_map/psum | solution.py:11
  150.2 151.0 %reduce-scatter.10.cloned.1.call-start = ((), (), s32[]{:S(2)}) async-start(), calls=%async_computation.9 | async-start | bytes 3342336 | tf_op jit(solution)/shard_map/reduce_scatter | solution.py:47
  225.3 154.3 %reduce-scatter.12.cloned.1.call-start = ((), (), s32[]{:S(2)}) async-start(), calls=%async_computation.10 | async-start | bytes 3342336 | tf_op jit(solution)/shard_map/reduce_scatter | solution.py:47
  234.4 224.1 %reduce-scatter.14.cloned.1.call-start = ((), (), s32[]{:S(2)}) async-start(), calls=%async_computation.11 | async-start | bytes 3342336 | tf_op jit(solution)/shard_map/reduce_scatter | solution.py:47
  243.6 136.0 %copy-start = (f32[3,512,512]{2,1,0:T(8,128)S(1)}, f32[3,512,512]{2,1,0:T(8,128)}, u32[]{:S(2)}) copy-start(f32[3,512,512]{2,1,0:T(8,128)} %param.7) | copy-start | bytes 9437188
  243.6 395.3 %all-reduce.5.cloned.1.call-start = ((), (), s32[]{:S(2)}) async-start(), calls=%async_computation.12 | async-start | bytes 12582912 | tf_op jit(solution)/shard_map/psum | solution.py:56
  301.2 159.9 %copy-start.16 = (f32[96,512]{1,0:T(8,128)S(1)}, f32[96,512]{1,0:T(8,128)}, u32[]{:S(2)}) copy-start(f32[96,512]{1,0:T(8,128)} %reduce-scatter.10.cloned.1.call-done) | copy-start | bytes 589828
  458.6 5.7 copy-start.22
  461.1 6.2 copy-start.17
  461.9 5.5 copy-start.19
  461.9 5.5 copy-start.21
  475.2 22.3 %all-to-all-start = ((f32[3,8,12,512]{3,2,0,1:T(8,128)}), f32[3,8,12,512]{3,2,0,1:T(8,128)}, u32[]{:S(2)}, u32[]{:S(2)}) async-start(f32[3,8,12,512]{3,2,0,1:T(8,128)} %copy.78), calls=%async_computation | async-start | bytes 1572864 | tf_op jit(solution)/shard_map/all_to_all | solution.py:80
  501.5 25.8 %all-to-all-start.1 = ((f32[3,16,12,512]{3,2,0,1:T(8,128)}), f32[3,16,12,512]{3,2,0,1:T(8,128)}, u32[]{:S(2)}, u32[]{:S(2)}) async-start(f32[3,16,12,512]{3,2,0,1:T(8,128)} %copy.80), calls=%async_computation.1 | async-start | bytes 3145728 | tf_op jit(solution)/shard_map/all_to_all | solution.py:86
  529.4 21.4 %all-to-all-start.2 = ((f32[3,8,12,512]{3,2,0,1:T(8,128)}), f32[3,8,12,512]{3,2,0,1:T(8,128)}, u32[]{:S(2)}, u32[]{:S(2)}) async-start(f32[3,8,12,512]{3,2,0,1:T(8,128)} %constant_dynamic-slice_fusion), calls=%async_computation.2 | async-start | bytes 1572864 | tf_op jit(solution)/shard_map/all_to_all | solution.py:88
  642.7 5.8 copy-start.1
  646.6 12.5 %copy-start.3 = (f32[512,512]{0,1:T(8,128)}, f32[512,512]{0,1:T(8,128)S(1)}, u32[]{:S(2)}) copy-start(f32[512,512]{0,1:T(8,128)S(1)} %fusion.18) | copy-start | bytes 3145732
  648.5 5.1 copy-start.6
  653.7 5.4 copy-start.4
  671.3 4.3 copy-start.2
  671.3 4.3 copy-start.12
  671.3 4.3 copy-start.15
  (10 other events, 25.4 us)
Sparse Core Ops, SparseCore 0:
  10.7 46.3 all-gather.5
  59.2 43.3 all-gather.3
  104.7 43.3 all-gather.7
  151.0 65.1 all-reduce.6
  225.4 75.7 reduce-scatter.9
  304.4 75.1 reduce-scatter.11
  383.4 75.0 reduce-scatter.13
  469.1 169.7 all-reduce.4
where the time goes:
time: 699 us; the launch traced here: 691 us
  waiting for transfers between devices  539 us (77%)
  matrix products  54.5 us (8%)
  local copies, waits for them, and re-layouts  36 us (5%)
  other arithmetic  26 us (4%)
  starting transfers between devices  21.2 us (3%)
  between operations  14.7 us (2%)
    reduce_scatter x3, waiting for transfers between devices, local(): lax.psum_scatter(matmul(ancestor_inverse, lower_cols), 'col', scatter_dim...  213 us
    all_gather x3, waiting for transfers between devices, local(): lower_rows = lax.all_gather(lower_part, 'col', axis=0, tiled=True)  132 us
    psum x1, waiting for transfers between devices, local(): summed = lax.psum(left_dot(lower_here, stacked), ('row', 'col'))  83.9 us
    psum x1, waiting for transfers between devices, broadcast(): return lax.psum(kept, axis)  66 us
    dot_general x11, matrix products, matmul(): return jnp.dot(left, right, precision=highest)  36 us
    all_to_all x1, waiting for transfers between devices, local(): lax.all_to_all(slotted, 'col', split_axis=1, concat_axis=1, tiled=True)  21 us
    dot_general x6, matrix products, left_dot(): lax.dot_general(left, right, (((0,), (0,)), ((), ())), precision=highest)  16.5 us
    all_to_all x1, waiting for transfers between devices, local(): lax.all_to_all(split_parts, 'row', split_axis=1, concat_axis=1, tiled=True)  15.6 us
  transfers between devices with their start and end apart: 11, of which 11 were waited for; matrix products, arithmetic and copies ran while one was open for 7% of the time, Pallas kernels for 0%

commit v1 on v0

--- a/solution.py
+++ b/solution.py
@@ -4,6 +4,39 @@
 from jax.sharding import PartitionSpec as P
 
 highest = lax.Precision.HIGHEST
+
+
+def bring_chains_for(sample, array_axis, vec):
+    t_next, last = (sample.shape[:array_axis], sample.shape[array_axis + 1 :])
+    work_now = sample.reshape(*t_next, vec, -1, *last)
+    return jnp.moveaxis(work_now, array_axis, 0)
+
+
+def array_save(row_data, on_dim):
+    row_data = jnp.moveaxis(row_data, 0, on_dim)
+    q_next = row_data.shape
+    return row_data.reshape(
+        *q_next[:on_dim], q_next[on_dim] * q_next[on_dim + 1], *q_next[on_dim + 2 :]
+    )
+
+
+def edit_widths(x_part, row_axis, work_x, block_in):
+    aux = lax.axis_size(row_axis)
+    z = lax.axis_index(row_axis)
+    mixed_arr, b_now = (aux, z)
+    z2 = bring_chains_for(x_part, work_x, mixed_arr)
+    cards = [z2[b_now]]
+    d = 1
+    while d < mixed_arr:
+        e_next = z2[(b_now + d) % mixed_arr]
+        state_next = lax.ppermute(
+            e_next, row_axis, [(j, (j + d) % mixed_arr) for j in range(mixed_arr)]
+        )
+        cards.append(state_next)
+        d += 1
+    w1 = jnp.stack(cards, 0)
+    z2 = w1[(b_now - jnp.arange(mixed_arr)) % mixed_arr]
+    return array_save(z2, block_in)
 
 
 def broadcast(value, axis, source):
@@ -85,7 +118,7 @@
     slotted = jnp.einsum("rc,nrqs->ncqs", onehot, held, precision=highest)
     arrived = lax.all_to_all(slotted, "col", split_axis=1, concat_axis=1, tiled=True)
     picked = lax.dynamic_slice_in_dim(arrived, col_index % ratio_cols * row_count, row_count, 1)
-    landed = lax.all_to_all(picked, "row", split_axis=1, concat_axis=1, tiled=True)
+    landed = edit_widths(picked, "row", 1, 1)
     mirrored_all = landed.reshape(nodes_total, piece_rows, sn_width)
     node_blocks = jnp.stack(
         [

time: 699 us -> 700 us (level)
  waiting for transfers between devices: 539 us -> 525 us
  local copies, waits for them, and re-layouts: 36 us -> 46.9 us
    ppermute x0 -> x7, starting transfers between devices: none -> 11.9 us  [edit_widths(): lax.ppermute(e_next, row_axis, [(j, (j + d) % mixed_arr) for j in range(m...]
    all_to_all x1 -> x0, starting transfers between devices: 9.01 us -> none  [local(): lax.all_to_all(picked, 'row', split_axis=1, concat_axis=1, tiled=True)]
    another operation x0 -> x3, local copies, waits for them, and re-layouts: none -> 7.49 us  [the longest x2 5.48 us: edit_widths(): w1 = jnp.stack(cards, 0)]
    unnamed x50 -> x71, local copies, waits for them, and re-layouts: 14.4 us -> 18 us
  transfers between devices with their start and end apart: 11 -> 17, of which waited for: 11 -> 11; matrix products, arithmetic and copies ran while one was open for 7% -> 8% of each run, Pallas kernels for 0% -> 0%
where the time goes in v1:
time: 700 us; the launch traced here: 692 us
  waiting for transfers between devices  525 us (75%)
  matrix products  54.5 us (8%)
  local copies, waits for them, and re-layouts  46.9 us (7%)
  other arithmetic  26 us (4%)
  starting transfers between devices  24.2 us (3%)
  between operations  15 us (2%)
    reduce_scatter x3, waiting for transfers between devices, local(): lax.psum_scatter(matmul(ancestor_inverse, lower_cols), 'col', scatter_dim...  213 us
    all_gather x3, waiting for transfers between devices, local(): lower_rows = lax.all_gather(lower_part, 'col', axis=0, tiled=True)  132 us
    psum x1, waiting for transfers between devices, local(): summed = lax.psum(left_dot(lower_here, stacked), ('row', 'col'))  80.8 us
    psum x1, waiting for transfers between devices, broadcast(): return lax.psum(kept, axis)  66 us
    dot_general x11, matrix products, matmul(): return jnp.dot(left, right, precision=highest)  36 us
    unnamed x71, local copies, waits for them, and re-layouts  18 us
    dot_general x6, matrix products, left_dot(): lax.dot_general(left, right, (((0,), (0,)), ((), ())), precision=highest)  16.4 us
    all_to_all x1, waiting for transfers between devices, local(): lax.all_to_all(slotted, 'col', split_axis=1, concat_axis=1, tiled=True)  16 us
  transfers between devices with their start and end apart: 17, of which 11 were waited for; matrix products, arithmetic and copies ran while one was open for 8% of the time, Pallas kernels for 0%

profile of v1, /device:TPU:1, one launch (start us, length us, event | category | flops | bytes accessed | tf_op | source)
XLA Modules:
  0.0 691.7 jit_solution(15029344123010885238)
XLA Ops:
  11.5 45.6 %all-gather.6.cloned.1.call-done = bf16[1536,512]{1,0:T(8,128)(2,1)} async-done(((bf16[96,512]{1,0:T(8,128)(2,1)}), bf16[1536,512]{1,0:T(8,128)(2,1)}) %all-gather.6.cloned.1.call-update) | async-done | bytes 1572880 | tf_op jit(solution)/shard_map/all_gather | solution.py:76
  59.2 43.3 %all-gather.4.cloned.1.call-done = bf16[1536,512]{1,0:T(8,128)(2,1)} async-done(((bf16[96,512]{1,0:T(8,128)(2,1)}), bf16[1536,512]{1,0:T(8,128)(2,1)}) %all-gather.4.cloned.1.call-update) | async-done | bytes 1572880 | tf_op jit(solution)/shard_map/all_gather | solution.py:76
  104.7 43.3 %all-gather.8.cloned.1.call-done = bf16[1536,512]{1,0:T(8,128)(2,1)} async-done(((bf16[96,512]{1,0:T(8,128)(2,1)}), bf16[1536,512]{1,0:T(8,128)(2,1)}) %all-gather.8.cloned.1.call-update) | async-done | bytes 1572880 | tf_op jit(solution)/shard_map/all_gather | solution.py:76
  150.3 66.0 %all-reduce.7.cloned.1.call-done = (bf16[768,512]{1,0:T(8,128)(2,1)}, bf16[768,512]{1,0:T(8,128)(2,1)}, bf16[768,512]{1,0:T(8,128)(2,1)}) async-done(((bf16[768,512]{1,0:T(8,128)(2,1)}, bf16[768,512]{1,0:T(8,128)(2,1)}, bf16[768,512]{1,0:T(8,128)(2,1)}), (bf16[768,512]{1,0:T(8,128)(2,1)}, bf16[768,512]{1,0:T(8,128)(2,1)}, bf16[768,512]{1,0:T(8,128)(2,1)})) %all-reduce.7.cloned.1.call-update) | async-done | bytes 2359312 | tf_op jit(solution)/shard_map/psum | solution.py:44
  216.2 6.7 convolution_bitcast_fusion.2
  225.3 6.7 convolution_bitcast_fusion.1
  234.5 6.7 convolution_bitcast_fusion
  244.1 57.1 %reduce-scatter.10.cloned.1.call-done = f32[96,512]{1,0:T(8,128)} async-done(((f32[1536,512]{1,0:T(8,128)}), f32[96,512]{1,0:T(8,128)}) %reduce-scatter.10.cloned.1.call-update) | async-done | bytes 196624 | tf_op jit(solution)/shard_map/reduce_scatter | solution.py:80
  301.2 78.3 %reduce-scatter.12.cloned.1.call-done = f32[96,512]{1,0:T(8,128)} async-done(((f32[1536,512]{1,0:T(8,128)}), f32[96,512]{1,0:T(8,128)}) %reduce-scatter.12.cloned.1.call-update) | async-done | bytes 196624 | tf_op jit(solution)/shard_map/reduce_scatter | solution.py:80
  381.3 77.1 %reduce-scatter.14.cloned.1.call-done = f32[96,512]{1,0:T(8,128)} async-done(((f32[1536,512]{1,0:T(8,128)}), f32[96,512]{1,0:T(8,128)}) %reduce-scatter.14.cloned.1.call-update) | async-done | bytes 196624 | tf_op jit(solution)/shard_map/reduce_scatter | solution.py:80
  464.1 3.1 fusion.38
  475.1 6.7 all-to-all-start
  481.8 15.5 %all-to-all-done = f32[3,8,12,512]{3,2,0,1:T(8,128)} async-done(((f32[3,8,12,512]{3,2,0,1:T(8,128)}), f32[3,8,12,512]{3,2,0,1:T(8,128)}, u32[]{:S(2)}, u32[]{:S(2)}) %all-to-all-start) | async-done | bytes 589856 | tf_op jit(solution)/shard_map/all_to_all | solution.py:113
  501.3 4.9 all-to-all-start.1
  511.1 16.0 %all-to-all-done.1 = f32[3,16,12,512]{3,2,0,1:T(8,128)} async-done(((f32[3,16,12,512]{3,2,0,1:T(8,128)}), f32[3,16,12,512]{3,2,0,1:T(8,128)}, u32[]{:S(2)}, u32[]{:S(2)}) %all-to-all-start.1) | async-done | bytes 1179680 | tf_op jit(solution)/shard_map/all_to_all | solution.py:119
  528.5 5.0 collective-permute-start
  546.5 3.1 stack.107
  558.8 80.8 %all-reduce.5.cloned.1.call-done = (f32[512,1536]{1,0:T(8,128)}, f32[512,512]{1,0:T(8,128)}, f32[512,1024]{0,1:T(8,128)}) async-done(((f32[512,1536]{1,0:T(8,128)}, f32[512,512]{1,0:T(8,128)}, f32[512,1024]{0,1:T(8,128)}), (f32[512,1536]{1,0:T(8,128)}, f32[512,512]{1,0:T(8,128)}, f32[512,1024]{0,1:T(8,128)})) %all-reduce.5.cloned.1.call-update) | async-done | bytes 6291472 | tf_op jit(solution)/shard_map/psum | solution.py:89
  639.6 3.8 bitcast_subtract_fusion.7
  654.3 3.0 fusion.2
  664.6 3.8 maximum_bitcast_fusion.1
  668.4 3.5 copy.168
  672.0 4.3 fusion.1
  679.7 4.9 pad_maximum_fusion
  (141 shorter events, 87.4 us)
Async XLA Ops:
  7.2 49.9 %all-gather.6.cloned.1.call-start = ((), (), s32[]{:S(2)}) async-start(), calls=%async_computation.6 | async-start | bytes 1671168 | tf_op jit(solution)/shard_map/all_gather | solution.py:76
  9.9 92.6 %all-gather.4.cloned.1.call-start = ((), (), s32[]{:S(2)}) async-start(), calls=%async_computation.5 | async-start | bytes 1671168 | tf_op jit(solution)/shard_map/all_gather | solution.py:76
  10.7 137.3 %all-gather.8.cloned.1.call-start = ((), (), s32[]{:S(2)}) async-start(), calls=%async_computation.7 | async-start | bytes 1671168 | tf_op jit(solution)/shard_map/all_gather | solution.py:76
  11.4 204.8 %all-reduce.7.cloned.1.call-start = ((), (), s32[]{:S(2)}) async-start(), calls=%async_computation.12 | async-start | bytes 4718592 | tf_op jit(solution)/shard_map/psum | solution.py:44
  150.2 151.0 %reduce-scatter.10.cloned.1.call-start = ((), (), s32[]{:S(2)}) async-start(), calls=%async_computation.8 | async-start | bytes 3342336 | tf_op jit(solution)/shard_map/reduce_scatter | solution.py:80
  225.3 154.3 %reduce-scatter.12.cloned.1.call-start = ((), (), s32[]{:S(2)}) async-start(), calls=%async_computation.9 | async-start | bytes 3342336 | tf_op jit(solution)/shard_map/reduce_scatter | solution.py:80
  234.4 224.0 %reduce-scatter.14.cloned.1.call-start = ((), (), s32[]{:S(2)}) async-start(), calls=%async_computation.10 | async-start | bytes 3342336 | tf_op jit(solution)/shard_map/reduce_scatter | solution.py:80
  243.5 136.0 %copy-start = (f32[3,512,512]{2,1,0:T(8,128)S(1)}, f32[3,512,512]{2,1,0:T(8,128)}, u32[]{:S(2)}) copy-start(f32[3,512,512]{2,1,0:T(8,128)} %param.7) | copy-start | bytes 9437188
  243.6 396.0 %all-reduce.5.cloned.1.call-start = ((), (), s32[]{:S(2)}) async-start(), calls=%async_computation.11 | async-start | bytes 12582912 | tf_op jit(solution)/shard_map/psum | solution.py:89
  301.2 159.8 %copy-start.16 = (f32[96,512]{1,0:T(8,128)S(1)}, f32[96,512]{1,0:T(8,128)}, u32[]{:S(2)}) copy-start(f32[96,512]{1,0:T(8,128)} %reduce-scatter.10.cloned.1.call-done) | copy-start | bytes 589828
  458.4 5.7 copy-start.22
  461.0 6.2 copy-start.17
  461.7 5.5 copy-start.19
  475.1 22.2 %all-to-all-start = ((f32[3,8,12,512]{3,2,0,1:T(8,128)}), f32[3,8,12,512]{3,2,0,1:T(8,128)}, u32[]{:S(2)}, u32[]{:S(2)}) async-start(f32[3,8,12,512]{3,2,0,1:T(8,128)} %copy.143), calls=%async_computation | async-start | bytes 1572864 | tf_op jit(solution)/shard_map/all_to_all | solution.py:113
  501.3 25.8 %all-to-all-start.1 = ((f32[3,16,12,512]{3,2,0,1:T(8,128)}), f32[3,16,12,512]{3,2,0,1:T(8,128)}, u32[]{:S(2)}, u32[]{:S(2)}) async-start(f32[3,16,12,512]{3,2,0,1:T(8,128)} %copy.145), calls=%async_computation.1 | async-start | bytes 3145728 | tf_op jit(solution)/shard_map/all_to_all | solution.py:119
  528.5 12.0 %collective-permute-start = (f32[3,1,12,512]{3,1,2,0:T(1,128)S(1)}, f32[3,1,12,512]{3,1,2,0:T(1,128)S(1)}, u32[]{:S(2)}, u32[]{:S(2)}) collective-permute-start(f32[3,1,12,512]{3,1,2,0:T(1,128)S(1)} %copy.183), channel_id=1, source_target_pairs={{0,16},{16,32},{32,48},{48,64},{64,80},{80,96},{96,112},{112,0},{1... | collective-permute-start | bytes 221192 | tf_op jit(solution)/shard_map/ppermute | solution.py:32
  533.6 7.0 %collective-permute-start.1 = (f32[3,1,12,512]{3,1,2,0:T(1,128)S(1)}, f32[3,1,12,512]{3,1,2,0:T(1,128)S(1)}, u32[]{:S(2)}, u32[]{:S(2)}) collective-permute-start(f32[3,1,12,512]{3,1,2,0:T(1,128)S(1)} %copy.184), channel_id=1, source_target_pairs={{0,32},{16,48},{32,64},{48,80},{64,96},{80,112},{96,0},{112,16},{1... | collective-permute-start | bytes 221192 | tf_op jit(solution)/shard_map/ppermute | solution.py:32
  533.8 9.5 %collective-permute-start.2 = (f32[3,1,12,512]{3,1,2,0:T(1,128)S(1)}, f32[3,1,12,512]{3,1,2,0:T(1,128)S(1)}, u32[]{:S(2)}, u32[]{:S(2)}) collective-permute-start(f32[3,1,12,512]{3,1,2,0:T(1,128)S(1)} %copy.185), channel_id=1, source_target_pairs={{0,48},{16,64},{32,80},{48,96},{64,112},{80,0},{96,16},{112,32},{1... | collective-permute-start | bytes 221192 | tf_op jit(solution)/shard_map/ppermute | solution.py:32
  535.2 8.2 %collective-permute-start.3 = (f32[3,1,12,512]{3,1,2,0:T(1,128)S(1)}, f32[3,1,12,512]{3,1,2,0:T(1,128)S(1)}, u32[]{:S(2)}, u32[]{:S(2)}) collective-permute-start(f32[3,1,12,512]{3,1,2,0:T(1,128)S(1)} %copy.186), channel_id=1, source_target_pairs={{0,64},{16,80},{32,96},{48,112},{64,0},{80,16},{96,32},{112,48},{1... | collective-permute-start | bytes 221192 | tf_op jit(solution)/shard_map/ppermute | solution.py:32
  537.6 6.3 collective-permute-start.4
  540.5 4.1 collective-permute-start.5
  540.6 4.6 collective-permute-start.6
  643.4 5.8 copy-start.1
  647.2 12.5 %copy-start.3 = (f32[512,512]{0,1:T(8,128)}, f32[512,512]{0,1:T(8,128)S(1)}, u32[]{:S(2)}) copy-start(f32[512,512]{0,1:T(8,128)S(1)} %fusion.18) | copy-start | bytes 3145732
  (23 other events, 62.6 us)
Sparse Core Ops, SparseCore 0:
  10.7 46.3 all-gather.5
  59.2 43.3 all-gather.3
  104.7 43.3 all-gather.7
  151.0 65.1 all-reduce.6
  225.4 75.7 reduce-scatter.9
  304.4 75.0 reduce-scatter.11
  383.4 74.9 reduce-scatter.13
  469.0 170.5 all-reduce.4
